TPU v7x, 32 devices: a whole 2x2x4 slice. The times are simulated.
32 devices in a mesh: flow: 32 (over z, y, x, core).
Axes of the slice: x: 2, y: 2, z: 4, core: 2. Of those that a mesh axis runs over, the one named last changes fastest.
Arguments:
- forcing: float32 [2, 12, 768, 1024], P(None, None, 'flow'), may hold values from -1000 to 1000
- viscosity: float32 [768, 1024], P('flow'), may hold values from 0.5 to 4
- friction: float32 [768, 1024], P('flow'), may hold values from 1 to 30
- rotation: float32 [768, 1024], P('flow'), may hold values from -2 to 2
- vertical: float32 [11, 768, 1024], P(None, 'flow'), may hold values from 2 to 20
- ice_mask: int32 [768, 1024], P('flow'), may hold values 0 or 1
- grounded: int32 [768, 1024], P('flow'), may hold values 0 or 1
Outputs:
- solution: float32 [2, 12, 768, 1024], P(None, None, 'flow')
- residual: float32 [2, 12, 768, 1024], P(None, None, 'flow')
All inputs are finite; a program needn't handle non-finite values. No bound on the sum of `ice_mask` or of `grounded` on one device may be relied on, other than what follows from the above.
Results may differ from a plain program's by a relative error of at most 0.0003.
Values sent between devices are 32-bit elements; how exact they have to be, the bound alone decides.
A program may use at most 192 MiB of HBM per device.

v0:
```python
import jax
import jax.numpy as jnp
from jax import lax
from jax.sharding import PartitionSpec as P

ITERS = 3


epsilon = 1e-06
relaxation = 0.5
reach_weights = (1.0, 0.6, 0.35, 0.2)


def extended(block, sides, width):
    for axis, dim in sides:
        count = lax.axis_size(axis)
        forward = [(i, i + 1) for i in range(count - 1)]
        backward = [(target, source) for source, target in forward]
        low = lax.ppermute(
            lax.slice_in_dim(block, block.shape[dim] - width, None, axis=dim), axis, forward
        )
        high = lax.ppermute(lax.slice_in_dim(block, 0, width, axis=dim), axis, backward)
        block = jnp.concatenate([low, block, high], axis=dim)
    return block


def layer_coefs(basal_drag, vertical):
    zero_plane = jnp.zeros_like(vertical[:1])
    upper_coef = jnp.concatenate([vertical, zero_plane], 0)
    lower_coef = jnp.concatenate([zero_plane, vertical], 0)
    bottom = jnp.concatenate([basal_drag[None], jnp.zeros_like(vertical)], 0)
    return (upper_coef, lower_coef, bottom)


def stencil_apply(padded, viscosity, basal_drag, rotation, ice_cover, vertical):
    row_count = padded.shape[2] - 8
    values = padded[:, :, 4 : 4 + row_count]
    horizontal = jnp.zeros_like(values)
    for order, weight in enumerate(reach_weights):
        offset = order + 1
        forward_cells = padded[:, :, 4 + offset : 4 + offset + row_count]
        backward_cells = padded[:, :, 4 - offset : 4 - offset + row_count]
        horizontal = horizontal + weight * (2.0 * values - forward_cells - backward_cells)
    padded_cross = jnp.pad(values, ((0, 0), (0, 0), (0, 0), (1, 1)))
    horizontal = horizontal + (2.0 * values - padded_cross[..., 2:] - padded_cross[..., :-2])
    upper_coef, lower_coef, bottom = layer_coefs(basal_drag, vertical)
    diagonal = upper_coef + lower_coef + bottom + relaxation * viscosity
    shifted_up = jnp.concatenate([values[:, 1:], jnp.zeros_like(values[:, :1])], 1)
    shifted_down = jnp.concatenate([jnp.zeros_like(values[:, :1]), values[:, :-1]], 1)
    turned = jnp.stack([values[1], -values[0]])
    stencil = (
        diagonal * values
        - upper_coef * shifted_up
        - lower_coef * shifted_down
        + rotation * turned
        + viscosity * horizontal
    )
    return jnp.where(ice_cover > 0.5, stencil, values)


def precondition(vector, viscosity, basal_drag, rotation, ice_cover, vertical):
    active = ice_cover > 0.5
    horiz_total = 2.0 * sum(reach_weights) + 2.0
    upper_coef, lower_coef, bottom = layer_coefs(basal_drag, vertical)
    real_part = upper_coef + lower_coef + bottom + relaxation * viscosity + horiz_total * viscosity
    real_part = jnp.where(active, real_part, jnp.ones_like(real_part))
    imag_part = jnp.where(active, rotation, jnp.zeros_like(rotation))
    coupling = jnp.where(active, vertical, jnp.zeros_like(vertical))
    layer_total = vector.shape[1]
    inv_real, inv_imag, carry_former, carry_latter = ([], [], [], [])
    for layer in range(layer_total):
        pivot_real = real_part[layer]
        pivot_imag = imag_part
        source_former = vector[0, layer]
        source_latter = vector[1, layer]
        if layer > 0:
            link = coupling[layer - 1]
            pivot_real = pivot_real - link * link * inv_real[layer - 1]
            pivot_imag = pivot_imag - link * link * inv_imag[layer - 1]
            source_former = source_former + link * carry_former[layer - 1]
            source_latter = source_latter + link * carry_latter[layer - 1]
        inverse_det = 1.0 / (pivot_real * pivot_real + pivot_imag * pivot_imag)
        entry_real = pivot_real * inverse_det
        entry_imag = -pivot_imag * inverse_det
        inv_real.append(entry_real)
        inv_imag.append(entry_imag)
        carry_former.append(entry_real * source_former + entry_imag * source_latter)
        carry_latter.append(entry_real * source_latter - entry_imag * source_former)
    result_former = [None] * layer_total
    result_latter = [None] * layer_total
    result_former[layer_total - 1] = carry_former[layer_total - 1]
    result_latter[layer_total - 1] = carry_latter[layer_total - 1]
    for layer in range(layer_total - 2, -1, -1):
        link = coupling[layer]
        pushed_former = link * result_former[layer + 1]
        pushed_latter = link * result_latter[layer + 1]
        result_former[layer] = (
            carry_former[layer] + inv_real[layer] * pushed_former + inv_imag[layer] * pushed_latter
        )
        result_latter[layer] = (
            carry_latter[layer] + inv_real[layer] * pushed_latter - inv_imag[layer] * pushed_former
        )
    solved = jnp.stack([jnp.stack(result_former), jnp.stack(result_latter)])
    return jnp.where(active, solved, vector)


def least_squares(columns, start):
    count_cols = len(columns)
    givens_rhs = [start] + [start * 0.0 for index in range(count_cols)]
    cosines, sines, upper_cols = ([], [], [])
    for column_index, column_in in enumerate(columns):
        column = list(column_in)
        for row_index in range(column_index):
            rotated_a = (
                cosines[row_index] * column[row_index] + sines[row_index] * column[row_index + 1]
            )
            rotated_b = (
                -sines[row_index] * column[row_index] + cosines[row_index] * column[row_index + 1]
            )
            column[row_index] = rotated_a
            column[row_index + 1] = rotated_b
        radius = jnp.sqrt(
            column[column_index] * column[column_index]
            + column[column_index + 1] * column[column_index + 1]
        )
        cosine = column[column_index] / radius
        sine_value = column[column_index + 1] / radius
        column[column_index] = radius
        cosines.append(cosine)
        sines.append(sine_value)
        upper_cols.append(column)
        next_rhs = -sine_value * givens_rhs[column_index]
        givens_rhs[column_index] = cosine * givens_rhs[column_index]
        givens_rhs[column_index + 1] = next_rhs
    factors = [None] * count_cols
    for column_index in range(count_cols - 1, -1, -1):
        accum = givens_rhs[column_index]
        for later in range(column_index + 1, count_cols):
            accum = accum - upper_cols[later][column_index] * factors[later]
        factors[column_index] = accum / upper_cols[column_index][column_index]
    return factors


def body(forcing, viscosity, friction, rotation, vertical, ice_mask, grounded):
    ice_cover = jnp.where(ice_mask > 0, jnp.ones_like(viscosity), jnp.zeros_like(viscosity))
    basal_drag = jnp.where(grounded > 0, friction, jnp.zeros_like(friction))
    squares_total = lax.psum(jnp.sum(forcing * forcing), "flow")
    load_norm = jnp.sqrt(squares_total + epsilon)
    local_coefs = (viscosity, basal_drag, rotation, ice_cover, vertical)
    halo_depth = 0

    def product(search):
        padded = extended(search, (("flow", 2),), 4)
        return (stencil_apply(padded, *local_coefs), 0)

    krylov = [(forcing / load_norm, halo_depth)]
    searches = []
    columns = []
    for iteration in range(ITERS):
        current, depth_from = krylov[iteration]
        search = precondition(current, *local_coefs)
        searches.append((search, depth_from))
        image, depth_to = product(search)
        aligned = [krylov[index][0] for index in range(iteration + 1)]
        column = []
        centre_image = image
        local_terms = [jnp.sum(centre_image * vector) for vector in aligned]
        local_terms.append(jnp.sum(centre_image * centre_image))
        products = lax.psum(jnp.stack(local_terms), "flow")
        remaining = products[len(aligned)]
        for index, vector in enumerate(aligned):
            image = image - products[index] * vector
            remaining = remaining - products[index] * products[index]
            column.append(products[index])
        new_norm = jnp.sqrt(jnp.maximum(remaining, 0.0) + epsilon)
        column.append(new_norm)
        columns.append(column)
        if iteration + 1 < ITERS:
            krylov.append((image / new_norm, depth_to))
    factors = least_squares(columns, load_norm)
    solution = factors[0] * searches[0][0]
    for index in range(1, ITERS):
        solution = solution + factors[index] * searches[index][0]
    applied, applied_depth = product(solution)
    residual = forcing - applied
    return (solution, residual)


def solution(mesh):
    return jax.shard_map(
        body,
        mesh=mesh,
        in_specs=(
            P(None, None, "flow", None),
            P("flow", None),
            P("flow", None),
            P("flow", None),
            P(None, "flow", None),
            P("flow", None),
            P("flow", None),
        ),
        out_specs=(P(None, None, "flow", None), P(None, None, "flow", None)),
        check_vma=False,
    )
```

profile of v0, /device:TPU:1, one launch (start us, length us, event | category | flops | bytes accessed | tf_op | source)
XLA Modules:
  0.0 325.0 jit_solution(11316784363831333662)
XLA Ops:
  0.7 1.8 broadcast_multiply_fusion.1
  2.4 2.9 multiply_reduce_fusion.9
  5.3 40.9 %psum.28 = f32[]{:T(128)} all-reduce(f32[]{:T(128)} %multiply_reduce_fusion.9), channel_id=1, replica_groups=mesh['flow'=32] {'flow'}, use_global_device_ids=true, to_apply=%region_1.2 | all-reduce | flops 1 | bytes 8 | tf_op jit(solution)/shard_map/psum | solution.py:147
  47.2 1.0 copy-done.86
  48.3 0.7 copy-done.110
  49.1 0.6 add_add_fusion
  50.4 0.5 fusion.147
  51.4 1.5 constant_dynamic-update-slice_fusion.11
  55.0 0.5 maximum_select_fusion
  55.9 0.5 copy-done.69
  56.8 3.2 collective-permute-start
  60.3 3.8 %collective-permute-start.1 = (f32[2,12,4,1024]{3,1,2,0:T(8,128)S(1)}, f32[2,12,4,1024]{3,1,2,0:T(8,128)S(1)}, u32[]{:S(2)}, u32[]{:S(2)}) collective-permute-start(f32[2,12,4,1024]{3,1,2,0:T(8,128)S(1)} %copy.92), channel_id=1, source_target_pairs={{0,1},{1,2},{2,3},{3,4},{4,5},{5,6},{6,7},{7,8},{8,9},{9,10},{10,1... | collective-permute-start | bytes 1179656 | tf_op jit(solution)/shard_map/ppermute | solution.py:19
  64.4 0.6 fusion.251
  65.0 6.1 %collective-permute-done = f32[2,12,4,1024]{3,1,2,0:T(8,128)S(1)} collective-permute-done((f32[2,12,4,1024]{3,1,2,0:T(8,128)S(1)}, f32[2,12,4,1024]{3,1,2,0:T(8,128)S(1)}, u32[]{:S(2)}, u32[]{:S(2)}) %collective-permute-start) | collective-permute-done | bytes 393248 | tf_op jit(solution)/shard_map/ppermute | solution.py:22
  71.4 2.5 collective-permute-done.1
  74.2 6.8 %multiply_reduce_fusion.8 = (f32[]{:T(128)}, f32[]{:T(128)}, f32[2,12,24,1024]{3,2,1,0:T(8,128)}) fusion(f32[2,12,24,1024]{3,2,1,0:T(8,128)S(1)} %maximum_select_fusion, f32[2,12,4,1024]{3,2,1,0:T(4,128)S(1)} %copy.93, f32[2,12,4,1024]{3,2,1,0:T(4,128)S(1)} %copy.91, f32[24,1024]{1,0:T(8,128)S(1)} %copy-done.101, ...), kind=kLoop, calls=%fused_computation.191 | loop fusion | flops 24772608 | bytes 18309132 | tf_op jit(solution)/shard_map/reduce_sum | solution.py:167
  81.0 1.3 pad_maximum_fusion.8
  82.3 39.2 %psum.29 = f32[2]{0:T(128)S(1)} all-reduce(f32[2]{0:T(128)S(1)} %pad_maximum_fusion.8), channel_id=1, replica_groups=mesh['flow'=32] {'flow'}, use_global_device_ids=true, to_apply=%region_4.5 | all-reduce | flops 2 | bytes 16 | tf_op jit(solution)/shard_map/psum | solution.py:169
  121.5 0.6 fusion.256
  124.2 3.0 subtract_divide_fusion.1
  127.5 0.5 fusion.123
  128.0 0.5 copy-done.62
  129.2 0.8 constant_dynamic-update-slice_fusion.35
  132.0 0.7 maximum_select_fusion.1
  132.7 0.5 copy-done.70
  133.6 1.3 copy.94
  134.9 3.4 %collective-permute-start.2 = (f32[2,12,4,1024]{3,1,2,0:T(8,128)}, f32[2,12,4,1024]{3,1,2,0:T(8,128)}, u32[]{:S(2)}, u32[]{:S(2)}) collective-permute-start(f32[2,12,4,1024]{3,1,2,0:T(8,128)} %copy.94), channel_id=1, source_target_pairs={{1,0},{2,1},{3,2},{4,3},{5,4},{6,5},{7,6},{8,7},{9,8},{10,9},{11,1... | collective-permute-start | bytes 1179656 | tf_op jit(solution)/shard_map/ppermute | solution.py:22
  138.3 1.0 copy.96
  139.4 3.8 %collective-permute-start.3 = (f32[2,12,4,1024]{3,1,2,0:T(8,128)}, f32[2,12,4,1024]{3,1,2,0:T(8,128)}, u32[]{:S(2)}, u32[]{:S(2)}) collective-permute-start(f32[2,12,4,1024]{3,1,2,0:T(8,128)} %copy.96), channel_id=1, source_target_pairs={{0,1},{1,2},{2,3},{3,4},{4,5},{5,6},{6,7},{7,8},{8,9},{9,10},{10,1... | collective-permute-start | bytes 1179656 | tf_op jit(solution)/shard_map/ppermute | solution.py:19
  143.2 1.7 fusion.249
  145.7 2.8 fusion.248
  148.4 0.6 collective-permute-done.2
  149.0 2.0 copy.95
  151.0 1.3 collective-permute-done.3
  152.3 1.3 copy.97
  153.7 7.9 %multiply_reduce_fusion.6 = (f32[]{:T(128)}, f32[]{:T(128)}, f32[]{:T(128)}, f32[2,12,24,1024]{3,2,1,0:T(8,128)}) fusion(f32[2,12,24,1024]{3,2,1,0:T(8,128)S(1)} %copy-done.2, f32[2,12,24,1024]{3,2,1,0:T(8,128)S(1)} %copy-done.10, f32[2,12,4,1024]{3,2,1,0:T(4,128)S(1)} %copy.97, f32[2,12,4,1024]{3,2,1,0:T(4,128)S(1)} %copy.95, ...), kind=kLoop, calls=%fused_computation.188 | loop fusion | flops 25952256 | bytes 20668432 | tf_op jit(solution)/shard_map/reduce_sum | solution.py:167
  161.6 1.9 pad_maximum_fusion.9
  163.5 39.2 %psum.30 = f32[3]{0:T(128)S(1)} all-reduce(f32[3]{0:T(128)S(1)} %pad_maximum_fusion.9), channel_id=1, replica_groups=mesh['flow'=32] {'flow'}, use_global_device_ids=true, to_apply=%region_8.9 | all-reduce | flops 3 | bytes 24 | tf_op jit(solution)/shard_map/psum | solution.py:169
  202.7 0.7 fusion.255
  206.7 4.9 %subtract_divide_fusion = f32[2,12,24,1024]{3,2,1,0:T(8,128)S(1)} fusion(f32[2,12,24,1024]{3,2,1,0:T(8,128)} %copy-done.1, f32[2,12,24,1024]{3,2,1,0:T(8,128)} %get-tuple-element.39, f32[]{:T(128)S(6)} %sqrt.24, f32[]{:T(128)} %bitcast.132, f32[]{:T(128)} %bitcast.131, f32[2,12,24,1024]{3,2,1,0:T(8,128)S(1)} %copy-done, f32[]{:T(128)S(6)} %sqrt.21), kind=kLoop, calls=%fused_computation.185 | loop fusion | flops 3538944 | bytes 9437200 | tf_op jit(solution)/shard_map/div | solution.py:179
  211.9 0.5 fusion.99
  212.4 0.4 copy-done.63
  213.4 0.8 constant_dynamic-update-slice_fusion.59
  216.1 0.5 maximum_select_fusion.2
  217.4 1.3 copy.100
  218.7 5.3 %collective-permute-start.5 = (f32[2,12,4,1024]{3,1,2,0:T(8,128)}, f32[2,12,4,1024]{3,1,2,0:T(8,128)}, u32[]{:S(2)}, u32[]{:S(2)}) collective-permute-start(f32[2,12,4,1024]{3,1,2,0:T(8,128)} %copy.100), channel_id=1, source_target_pairs={{0,1},{1,2},{2,3},{3,4},{4,5},{5,6},{6,7},{7,8},{8,9},{9,10},{10,1... | collective-permute-start | bytes 1179656 | tf_op jit(solution)/shard_map/ppermute | solution.py:19
  224.0 1.0 copy.98
  225.0 1.9 collective-permute-start.4
  226.9 1.7 fusion.246
  231.3 2.7 fusion.245
  234.1 2.1 copy.101
  236.2 1.5 collective-permute-done.4
  237.6 1.3 copy.99
  239.0 7.5 %multiply_reduce_fusion.3 = (f32[]{:T(128)}, f32[]{:T(128)}, f32[]{:T(128)}, f32[]{:T(128)}) fusion(f32[2,12,24,1024]{3,2,1,0:T(8,128)S(1)} %copy-done.5, f32[2,12,24,1024]{3,2,1,0:T(8,128)S(1)} %copy-done.3, f32[2,12,24,1024]{3,2,1,0:T(8,128)S(1)} %copy-done.8, f32[2,12,4,1024]{3,2,1,0:T(4,128)S(1)} %copy.101, f32[2,12,4,1024]{3,2,1,0:T(4,128)S(1)} %copy.99, ...), kind=kLoop, calls=%fused_computation.184 | loop fusion | flops 27131904 | bytes 20668436 | tf_op jit(solution)/shard_map/reduce_sum | solution.py:167
  246.5 2.5 pad_maximum_fusion.10
  249.0 38.3 %psum.31 = f32[4]{0:T(128)S(1)} all-reduce(f32[4]{0:T(128)S(1)} %pad_maximum_fusion.10), channel_id=1, replica_groups=mesh['flow'=32] {'flow'}, use_global_device_ids=true, to_apply=%region_13.14 | all-reduce | flops 4 | bytes 32 | tf_op jit(solution)/shard_map/psum | solution.py:169
  287.3 0.6 fusion.254
  295.9 5.3 %multiply_add_fusion = f32[2,12,24,1024]{3,2,1,0:T(8,128)S(1)} fusion(f32[]{:T(128)S(6)} %div.125, f32[]{:T(128)S(6)} %div.126, f32[]{:T(128)S(6)} %div.127, f32[2,12,24,1024]{3,2,1,0:T(8,128)} %copy-done.4, f32[1,12,24,1024]{3,2,1,0:T(8,128)} %bitcast.1892, f32[1,12,24,1024]{3,2,1,0:T(8,128)} %bitcast.1900, pred[24,1024]{1,0:T(8,128)(4,1)S(1)} %copy-done.97, ...), kind=kLoop, calls=%fused_computation.180 | loop fusion | flops 7077888 | bytes 16539664 | tf_op jit(solution)/shard_map/add | solution.py:183
  301.6 3.4 %collective-permute-start.6 = (f32[2,12,4,1024]{3,1,2,0:T(8,128)S(1)}, f32[2,12,4,1024]{3,1,2,0:T(8,128)S(1)}, u32[]{:S(2)}, u32[]{:S(2)}) collective-permute-start(f32[2,12,4,1024]{3,1,2,0:T(8,128)S(1)} %copy.102), channel_id=1, source_target_pairs={{1,0},{2,1},{3,2},{4,3},{5,4},{6,5},{7,6},{8,7},{9,8},{10,9},{11,1... | collective-permute-start | bytes 1179656 | tf_op jit(solution)/shard_map/ppermute | solution.py:22
  305.3 3.8 %collective-permute-start.7 = (f32[2,12,4,1024]{3,1,2,0:T(8,128)S(1)}, f32[2,12,4,1024]{3,1,2,0:T(8,128)S(1)}, u32[]{:S(2)}, u32[]{:S(2)}) collective-permute-start(f32[2,12,4,1024]{3,1,2,0:T(8,128)S(1)} %copy.104), channel_id=1, source_target_pairs={{0,1},{1,2},{2,3},{3,4},{4,5},{5,6},{6,7},{7,8},{8,9},{9,10},{10,1... | collective-permute-start | bytes 1179656 | tf_op jit(solution)/shard_map/ppermute | solution.py:19
  309.4 0.6 fusion.242
  310.0 5.8 %collective-permute-done.6 = f32[2,12,4,1024]{3,1,2,0:T(8,128)S(1)} collective-permute-done((f32[2,12,4,1024]{3,1,2,0:T(8,128)S(1)}, f32[2,12,4,1024]{3,1,2,0:T(8,128)S(1)}, u32[]{:S(2)}, u32[]{:S(2)}) %collective-permute-start.6) | collective-permute-done | bytes 393248 | tf_op jit(solution)/shard_map/ppermute | solution.py:22
  316.0 2.7 collective-permute-done.7
  319.0 6.0 %fusion.24 = f32[2,12,24,1024]{3,2,1,0:T(8,128)} fusion(f32[2,12,24,1024]{3,2,1,0:T(8,128)S(1)} %copy-done, f32[2,12,24,1024]{3,2,1,0:T(8,128)S(1)} %multiply_add_fusion, f32[2,12,4,1024]{3,2,1,0:T(4,128)S(1)} %copy.105, f32[2,12,4,1024]{3,2,1,0:T(4,128)S(1)} %copy.103, f32[1,12,24,1024]{3,2,1,0:T(8,128)S(1)} %get-tuple-element.148, ...), kind=kLoop, calls=%fused_computation.80 | loop fusion | flops 22413312 | bytes 18309120 | tf_op jit(solution)/shard_map/sub | solution.py:185
  (291 shorter events, 13.0 us)
Async XLA Ops:
  0.6 46.3 %copy-start = (f32[2,12,24,1024]{3,2,1,0:T(8,128)S(1)}, f32[2,12,24,1024]{3,2,1,0:T(8,128)}, u32[]{:S(2)}) copy-start(f32[2,12,24,1024]{3,2,1,0:T(8,128)} %param.7) | copy-start | bytes 7077892
  0.6 4.7 %copy-start.108 = (s32[24,1024]{1,0:T(8,128)S(1)}, s32[24,1024]{1,0:T(8,128)}, u32[]{:S(2)}) copy-start(s32[24,1024]{1,0:T(8,128)} %param.12) | copy-start | bytes 294916
  5.3 43.0 %copy-start.93 = (pred[24,1024]{1,0:T(8,128)(4,1)}, pred[24,1024]{1,0:T(8,128)(4,1)S(1)}, u32[]{:S(2)}) copy-start(pred[24,1024]{1,0:T(8,128)(4,1)S(1)} %select_compare_fusion) | copy-start | bytes 73732
  49.7 24.5 %copy-start.32 = (f32[12,24,1024]{2,1,0:T(8,128)}, f32[12,24,1024]{2,1,0:T(8,128)S(1)}, u32[]{:S(2)}) copy-start(f32[12,24,1024]{2,1,0:T(8,128)S(1)} %get-tuple-element.169) | copy-start | bytes 3538948
  49.7 24.5 %copy-start.36 = (f32[12,24,1024]{2,1,0:T(8,128)}, f32[12,24,1024]{2,1,0:T(8,128)S(1)}, u32[]{:S(2)}) copy-start(f32[12,24,1024]{2,1,0:T(8,128)S(1)} %get-tuple-element.174) | copy-start | bytes 3538948
  49.7 24.5 %copy-start.40 = (f32[12,24,1024]{2,1,0:T(8,128)}, f32[12,24,1024]{2,1,0:T(8,128)S(1)}, u32[]{:S(2)}) copy-start(f32[12,24,1024]{2,1,0:T(8,128)S(1)} %get-tuple-element.175) | copy-start | bytes 3538948
  50.3 3.3 %copy-start.11 = (f32[24,1024]{1,0:T(8,128)}, f32[24,1024]{1,0:T(8,128)S(1)}, u32[]{:S(2)}) copy-start(f32[24,1024]{1,0:T(8,128)S(1)} %get-tuple-element.101) | copy-start | bytes 294916
  50.4 3.3 %copy-start.14 = (f32[24,1024]{1,0:T(8,128)}, f32[24,1024]{1,0:T(8,128)S(1)}, u32[]{:S(2)}) copy-start(f32[24,1024]{1,0:T(8,128)S(1)} %get-tuple-element.102) | copy-start | bytes 294916
  51.0 3.5 %copy-start.20 = (f32[24,1024]{1,0:T(8,128)}, f32[24,1024]{1,0:T(8,128)S(1)}, u32[]{:S(2)}) copy-start(f32[24,1024]{1,0:T(8,128)S(1)} %get-tuple-element.79) | copy-start | bytes 294916
  51.0 3.5 %copy-start.23 = (f32[24,1024]{1,0:T(8,128)}, f32[24,1024]{1,0:T(8,128)S(1)}, u32[]{:S(2)}) copy-start(f32[24,1024]{1,0:T(8,128)S(1)} %get-tuple-element.80) | copy-start | bytes 294916
  51.0 3.5 %copy-start.26 = (f32[24,1024]{1,0:T(8,128)}, f32[24,1024]{1,0:T(8,128)S(1)}, u32[]{:S(2)}) copy-start(f32[24,1024]{1,0:T(8,128)S(1)} %get-tuple-element.83) | copy-start | bytes 294916
  51.0 3.5 %copy-start.29 = (f32[24,1024]{1,0:T(8,128)}, f32[24,1024]{1,0:T(8,128)S(1)}, u32[]{:S(2)}) copy-start(f32[24,1024]{1,0:T(8,128)S(1)} %get-tuple-element.84) | copy-start | bytes 294916
  56.8 14.3 %collective-permute-start = (f32[2,12,4,1024]{3,1,2,0:T(8,128)S(1)}, f32[2,12,4,1024]{3,1,2,0:T(8,128)S(1)}, u32[]{:S(2)}, u32[]{:S(2)}) collective-permute-start(f32[2,12,4,1024]{3,1,2,0:T(8,128)S(1)} %copy.90), channel_id=1, source_target_pairs={{1,0},{2,1},{3,2},{4,3},{5,4},{6,5},{7,6},{8,7},{9,8},{10,9},{11,1... | collective-permute-start | bytes 1179656 | tf_op jit(solution)/shard_map/ppermute | solution.py:22
  60.3 13.7 %collective-permute-start.1 = (f32[2,12,4,1024]{3,1,2,0:T(8,128)S(1)}, f32[2,12,4,1024]{3,1,2,0:T(8,128)S(1)}, u32[]{:S(2)}, u32[]{:S(2)}) collective-permute-start(f32[2,12,4,1024]{3,1,2,0:T(8,128)S(1)} %copy.92), channel_id=1, source_target_pairs={{0,1},{1,2},{2,3},{3,4},{4,5},{5,6},{6,7},{7,8},{8,9},{9,10},{10,1... | collective-permute-start | bytes 1179656 | tf_op jit(solution)/shard_map/ppermute | solution.py:19
  64.4 9.8 %copy-start.101 = (f32[24,1024]{1,0:T(8,128)S(1)}, f32[24,1024]{1,0:T(8,128)}, u32[]{:S(2)}) copy-start(f32[24,1024]{1,0:T(8,128)} %param.8) | copy-start | bytes 294916
  127.4 4.4 %copy-start.1 = (f32[2,12,24,1024]{3,2,1,0:T(8,128)}, f32[2,12,24,1024]{3,2,1,0:T(8,128)S(1)}, u32[]{:S(2)}) copy-start(f32[2,12,24,1024]{3,2,1,0:T(8,128)S(1)} %subtract_divide_fusion.1) | copy-start | bytes 7077892
  133.4 9.7 %copy-start.9 = (f32[2,12,24,1024]{3,2,1,0:T(8,128)}, f32[2,12,24,1024]{3,2,1,0:T(8,128)S(1)}, u32[]{:S(2)}) copy-start(f32[2,12,24,1024]{3,2,1,0:T(8,128)S(1)} %maximum_select_fusion.1) | copy-start | bytes 7077892
  134.9 14.1 %collective-permute-start.2 = (f32[2,12,4,1024]{3,1,2,0:T(8,128)}, f32[2,12,4,1024]{3,1,2,0:T(8,128)}, u32[]{:S(2)}, u32[]{:S(2)}) collective-permute-start(f32[2,12,4,1024]{3,1,2,0:T(8,128)} %copy.94), channel_id=1, source_target_pairs={{1,0},{2,1},{3,2},{4,3},{5,4},{6,5},{7,6},{8,7},{9,8},{10,9},{11,1... | collective-permute-start | bytes 1179656 | tf_op jit(solution)/shard_map/ppermute | solution.py:22
  139.4 13.0 %collective-permute-start.3 = (f32[2,12,4,1024]{3,1,2,0:T(8,128)}, f32[2,12,4,1024]{3,1,2,0:T(8,128)}, u32[]{:S(2)}, u32[]{:S(2)}) collective-permute-start(f32[2,12,4,1024]{3,1,2,0:T(8,128)} %copy.96), channel_id=1, source_target_pairs={{0,1},{1,2},{2,3},{3,4},{4,5},{5,6},{6,7},{7,8},{8,9},{9,10},{10,1... | collective-permute-start | bytes 1179656 | tf_op jit(solution)/shard_map/ppermute | solution.py:19
  145.6 8.1 %copy-start.2 = (f32[2,12,24,1024]{3,2,1,0:T(8,128)S(1)}, f32[2,12,24,1024]{3,2,1,0:T(8,128)}, u32[]{:S(2)}) copy-start(f32[2,12,24,1024]{3,2,1,0:T(8,128)} %copy-done.1) | copy-start | bytes 7077892
  145.6 8.1 %copy-start.10 = (f32[2,12,24,1024]{3,2,1,0:T(8,128)S(1)}, f32[2,12,24,1024]{3,2,1,0:T(8,128)}, u32[]{:S(2)}) copy-start(f32[2,12,24,1024]{3,2,1,0:T(8,128)} %copy-done.9) | copy-start | bytes 7077892
  145.6 8.1 %copy-start.37 = (f32[12,24,1024]{2,1,0:T(8,128)S(1)}, f32[12,24,1024]{2,1,0:T(8,128)}, u32[]{:S(2)}) copy-start(f32[12,24,1024]{2,1,0:T(8,128)} %copy-done.36) | copy-start | bytes 3538948
  145.6 8.1 %copy-start.41 = (f32[12,24,1024]{2,1,0:T(8,128)S(1)}, f32[12,24,1024]{2,1,0:T(8,128)}, u32[]{:S(2)}) copy-start(f32[12,24,1024]{2,1,0:T(8,128)} %copy-done.40) | copy-start | bytes 3538948
  145.6 8.1 %copy-start.85 = (f32[1,12,24,1024]{3,2,1,0:T(8,128)S(1)}, f32[1,12,24,1024]{3,2,1,0:T(8,128)}, u32[]{:S(2)}) copy-start(f32[1,12,24,1024]{3,2,1,0:T(8,128)} %get-tuple-element.159) | copy-start | bytes 3538948
  145.6 8.1 %copy-start.96 = (pred[24,1024]{1,0:T(8,128)(4,1)S(1)}, pred[24,1024]{1,0:T(8,128)(4,1)}, u32[]{:S(2)}) copy-start(pred[24,1024]{1,0:T(8,128)(4,1)} %copy-done.93) | copy-start | bytes 73732
  145.6 8.1 %copy-start.99 = (f32[24,1024]{1,0:T(8,128)S(1)}, f32[24,1024]{1,0:T(8,128)}, u32[]{:S(2)}) copy-start(f32[24,1024]{1,0:T(8,128)} %param.10) | copy-start | bytes 294916
  145.7 8.1 %copy-start.102 = (f32[24,1024]{1,0:T(8,128)S(1)}, f32[24,1024]{1,0:T(8,128)}, u32[]{:S(2)}) copy-start(f32[24,1024]{1,0:T(8,128)} %param.8) | copy-start | bytes 294916
  148.4 5.3 %copy-start.33 = (f32[12,24,1024]{2,1,0:T(8,128)S(1)}, f32[12,24,1024]{2,1,0:T(8,128)}, u32[]{:S(2)}) copy-start(f32[12,24,1024]{2,1,0:T(8,128)} %copy-done.32) | copy-start | bytes 3538948
  206.6 5.1 %copy-start.13 = (f32[24,1024]{1,0:T(8,128)S(1)}, f32[24,1024]{1,0:T(8,128)}, u32[]{:S(2)}) copy-start(f32[24,1024]{1,0:T(8,128)} %copy-done.11) | copy-start | bytes 294916
  206.6 5.1 %copy-start.16 = (f32[24,1024]{1,0:T(8,128)S(1)}, f32[24,1024]{1,0:T(8,128)}, u32[]{:S(2)}) copy-start(f32[24,1024]{1,0:T(8,128)} %copy-done.14) | copy-start | bytes 294916
  206.6 5.1 %copy-start.19 = (f32[24,1024]{1,0:T(8,128)S(1)}, f32[24,1024]{1,0:T(8,128)}, u32[]{:S(2)}) copy-start(f32[24,1024]{1,0:T(8,128)} %copy-done.17) | copy-start | bytes 294916
  206.6 5.1 %copy-start.22 = (f32[24,1024]{1,0:T(8,128)S(1)}, f32[24,1024]{1,0:T(8,128)}, u32[]{:S(2)}) copy-start(f32[24,1024]{1,0:T(8,128)} %copy-done.20) | copy-start | bytes 294916
  206.6 5.1 %copy-start.25 = (f32[24,1024]{1,0:T(8,128)S(1)}, f32[24,1024]{1,0:T(8,128)}, u32[]{:S(2)}) copy-start(f32[24,1024]{1,0:T(8,128)} %copy-done.23) | copy-start | bytes 294916
  206.6 5.1 %copy-start.28 = (f32[24,1024]{1,0:T(8,128)S(1)}, f32[24,1024]{1,0:T(8,128)}, u32[]{:S(2)}) copy-start(f32[24,1024]{1,0:T(8,128)} %copy-done.26) | copy-start | bytes 294916
  206.6 5.1 %copy-start.31 = (f32[24,1024]{1,0:T(8,128)S(1)}, f32[24,1024]{1,0:T(8,128)}, u32[]{:S(2)}) copy-start(f32[24,1024]{1,0:T(8,128)} %copy-done.29) | copy-start | bytes 294916
  206.6 5.1 %copy-start.45 = (f32[24,1024]{1,0:T(8,128)S(1)}, f32[24,1024]{1,0:T(8,128)}, u32[]{:S(2)}) copy-start(f32[24,1024]{1,0:T(8,128)} %copy-done.43) | copy-start | bytes 294916
  206.6 5.1 %copy-start.48 = (f32[24,1024]{1,0:T(8,128)S(1)}, f32[24,1024]{1,0:T(8,128)}, u32[]{:S(2)}) copy-start(f32[24,1024]{1,0:T(8,128)} %copy-done.46) | copy-start | bytes 294916
  206.6 5.1 %copy-start.51 = (f32[24,1024]{1,0:T(8,128)S(1)}, f32[24,1024]{1,0:T(8,128)}, u32[]{:S(2)}) copy-start(f32[24,1024]{1,0:T(8,128)} %copy-done.49) | copy-start | bytes 294916
  206.7 5.1 %copy-start.54 = (f32[24,1024]{1,0:T(8,128)S(1)}, f32[24,1024]{1,0:T(8,128)}, u32[]{:S(2)}) copy-start(f32[24,1024]{1,0:T(8,128)} %copy-done.52) | copy-start | bytes 294916
  206.7 5.1 %copy-start.57 = (f32[24,1024]{1,0:T(8,128)S(1)}, f32[24,1024]{1,0:T(8,128)}, u32[]{:S(2)}) copy-start(f32[24,1024]{1,0:T(8,128)} %copy-done.55) | copy-start | bytes 294916
  206.7 5.1 %copy-start.60 = (f32[24,1024]{1,0:T(8,128)S(1)}, f32[24,1024]{1,0:T(8,128)}, u32[]{:S(2)}) copy-start(f32[24,1024]{1,0:T(8,128)} %copy-done.58) | copy-start | bytes 294916
  206.7 5.1 %copy-start.81 = (f32[24,1024]{1,0:T(8,128)S(1)}, f32[24,1024]{1,0:T(8,128)}, u32[]{:S(2)}) copy-start(f32[24,1024]{1,0:T(8,128)} %copy-done.79) | copy-start | bytes 294916
  206.7 5.1 %copy-start.84 = (f32[24,1024]{1,0:T(8,128)S(1)}, f32[24,1024]{1,0:T(8,128)}, u32[]{:S(2)}) copy-start(f32[24,1024]{1,0:T(8,128)} %copy-done.82) | copy-start | bytes 294916
  206.7 5.1 %copy-start.89 = (f32[24,1024]{1,0:T(8,128)S(1)}, f32[24,1024]{1,0:T(8,128)}, u32[]{:S(2)}) copy-start(f32[24,1024]{1,0:T(8,128)} %copy-done.87) | copy-start | bytes 294916
  206.7 5.1 %copy-start.92 = (f32[24,1024]{1,0:T(8,128)S(1)}, f32[24,1024]{1,0:T(8,128)}, u32[]{:S(2)}) copy-start(f32[24,1024]{1,0:T(8,128)} %copy-done.90) | copy-start | bytes 294916
  206.7 5.1 %copy-start.105 = (f32[24,1024]{1,0:T(8,128)S(1)}, f32[24,1024]{1,0:T(8,128)}, u32[]{:S(2)}) copy-start(f32[24,1024]{1,0:T(8,128)} %get-tuple-element.76) | copy-start | bytes 294916
  206.7 5.1 %copy-start.107 = (f32[24,1024]{1,0:T(8,128)S(1)}, f32[24,1024]{1,0:T(8,128)}, u32[]{:S(2)}) copy-start(f32[24,1024]{1,0:T(8,128)} %get-tuple-element.77) | copy-start | bytes 294916
  211.9 4.0 %copy-start.4 = (f32[2,12,24,1024]{3,2,1,0:T(8,128)}, f32[2,12,24,1024]{3,2,1,0:T(8,128)S(1)}, u32[]{:S(2)}) copy-start(f32[2,12,24,1024]{3,2,1,0:T(8,128)S(1)} %subtract_divide_fusion) | copy-start | bytes 7077892
  217.2 9.7 %copy-start.7 = (f32[2,12,24,1024]{3,2,1,0:T(8,128)}, f32[2,12,24,1024]{3,2,1,0:T(8,128)S(1)}, u32[]{:S(2)}) copy-start(f32[2,12,24,1024]{3,2,1,0:T(8,128)S(1)} %maximum_select_fusion.2) | copy-start | bytes 7077892
  218.7 15.4 %collective-permute-start.5 = (f32[2,12,4,1024]{3,1,2,0:T(8,128)}, f32[2,12,4,1024]{3,1,2,0:T(8,128)}, u32[]{:S(2)}, u32[]{:S(2)}) collective-permute-start(f32[2,12,4,1024]{3,1,2,0:T(8,128)} %copy.100), channel_id=1, source_target_pairs={{0,1},{1,2},{2,3},{3,4},{4,5},{5,6},{6,7},{7,8},{8,9},{9,10},{10,1... | collective-permute-start | bytes 1179656 | tf_op jit(solution)/shard_map/ppermute | solution.py:19
  225.0 12.6 %collective-permute-start.4 = (f32[2,12,4,1024]{3,1,2,0:T(8,128)}, f32[2,12,4,1024]{3,1,2,0:T(8,128)}, u32[]{:S(2)}, u32[]{:S(2)}) collective-permute-start(f32[2,12,4,1024]{3,1,2,0:T(8,128)} %copy.98), channel_id=1, source_target_pairs={{1,0},{2,1},{3,2},{4,3},{5,4},{6,5},{7,6},{8,7},{9,8},{10,9},{11,1... | collective-permute-start | bytes 1179656 | tf_op jit(solution)/shard_map/ppermute | solution.py:22
  231.2 7.7 %copy-start.3 = (f32[2,12,24,1024]{3,2,1,0:T(8,128)S(1)}, f32[2,12,24,1024]{3,2,1,0:T(8,128)}, u32[]{:S(2)}) copy-start(f32[2,12,24,1024]{3,2,1,0:T(8,128)} %copy-done.1) | copy-start | bytes 7077892
  231.2 7.7 %copy-start.5 = (f32[2,12,24,1024]{3,2,1,0:T(8,128)S(1)}, f32[2,12,24,1024]{3,2,1,0:T(8,128)}, u32[]{:S(2)}) copy-start(f32[2,12,24,1024]{3,2,1,0:T(8,128)} %copy-done.4) | copy-start | bytes 7077892
  231.3 7.7 %copy-start.8 = (f32[2,12,24,1024]{3,2,1,0:T(8,128)S(1)}, f32[2,12,24,1024]{3,2,1,0:T(8,128)}, u32[]{:S(2)}) copy-start(f32[2,12,24,1024]{3,2,1,0:T(8,128)} %copy-done.7) | copy-start | bytes 7077892
  231.3 7.7 %copy-start.38 = (f32[12,24,1024]{2,1,0:T(8,128)S(1)}, f32[12,24,1024]{2,1,0:T(8,128)}, u32[]{:S(2)}) copy-start(f32[12,24,1024]{2,1,0:T(8,128)} %copy-done.36) | copy-start | bytes 3538948
  231.3 7.7 %copy-start.100 = (f32[24,1024]{1,0:T(8,128)S(1)}, f32[24,1024]{1,0:T(8,128)}, u32[]{:S(2)}) copy-start(f32[24,1024]{1,0:T(8,128)} %param.10) | copy-start | bytes 294916
  231.3 7.7 %copy-start.103 = (f32[24,1024]{1,0:T(8,128)S(1)}, f32[24,1024]{1,0:T(8,128)}, u32[]{:S(2)}) copy-start(f32[24,1024]{1,0:T(8,128)} %param.8) | copy-start | bytes 294916
  234.1 4.9 %copy-start.34 = (f32[12,24,1024]{2,1,0:T(8,128)S(1)}, f32[12,24,1024]{2,1,0:T(8,128)}, u32[]{:S(2)}) copy-start(f32[12,24,1024]{2,1,0:T(8,128)} %copy-done.32) | copy-start | bytes 3538948
  301.2 17.8 %copy-start.6 = (f32[2,12,24,1024]{3,2,1,0:T(8,128)}, f32[2,12,24,1024]{3,2,1,0:T(8,128)S(1)}, u32[]{:S(2)}) copy-start(f32[2,12,24,1024]{3,2,1,0:T(8,128)S(1)} %multiply_add_fusion) | copy-start | bytes 7077892
  301.6 14.1 %collective-permute-start.6 = (f32[2,12,4,1024]{3,1,2,0:T(8,128)S(1)}, f32[2,12,4,1024]{3,1,2,0:T(8,128)S(1)}, u32[]{:S(2)}, u32[]{:S(2)}) collective-permute-start(f32[2,12,4,1024]{3,1,2,0:T(8,128)S(1)} %copy.102), channel_id=1, source_target_pairs={{1,0},{2,1},{3,2},{4,3},{5,4},{6,5},{7,6},{8,7},{9,8},{10,9},{11,1... | collective-permute-start | bytes 1179656 | tf_op jit(solution)/shard_map/ppermute | solution.py:22
  305.3 13.5 %collective-permute-start.7 = (f32[2,12,4,1024]{3,1,2,0:T(8,128)S(1)}, f32[2,12,4,1024]{3,1,2,0:T(8,128)S(1)}, u32[]{:S(2)}, u32[]{:S(2)}) collective-permute-start(f32[2,12,4,1024]{3,1,2,0:T(8,128)S(1)} %copy.104), channel_id=1, source_target_pairs={{0,1},{1,2},{2,3},{3,4},{4,5},{5,6},{6,7},{7,8},{8,9},{9,10},{10,1... | collective-permute-start | bytes 1179656 | tf_op jit(solution)/shard_map/ppermute | solution.py:19
  309.4 9.6 %copy-start.39 = (f32[12,24,1024]{2,1,0:T(8,128)S(1)}, f32[12,24,1024]{2,1,0:T(8,128)}, u32[]{:S(2)}) copy-start(f32[12,24,1024]{2,1,0:T(8,128)} %copy-done.36) | copy-start | bytes 3538948
  309.4 9.6 %copy-start.42 = (f32[12,24,1024]{2,1,0:T(8,128)S(1)}, f32[12,24,1024]{2,1,0:T(8,128)}, u32[]{:S(2)}) copy-start(f32[12,24,1024]{2,1,0:T(8,128)} %copy-done.40) | copy-start | bytes 3538948
  310.0 9.0 %copy-start.35 = (f32[12,24,1024]{2,1,0:T(8,128)S(1)}, f32[12,24,1024]{2,1,0:T(8,128)}, u32[]{:S(2)}) copy-start(f32[12,24,1024]{2,1,0:T(8,128)} %copy-done.32) | copy-start | bytes 3538948
  (58 other events, 119.8 us)
where the time goes:
time: 327 us; the launch traced here: 325 us
  blocking collectives  158 us (48%)
  other arithmetic  68.1 us (21%)
  local copies, waits for them, and re-layouts  30.4 us (9%)
  starting transfers between devices  28.5 us (9%)
  waiting for transfers between devices  20.5 us (6%)
  between operations  19.9 us (6%)
    psum x3, blocking collectives, body(): products = lax.psum(jnp.stack(local_terms), 'flow')  117 us
    psum x1, blocking collectives, body(): squares_total = lax.psum(jnp.sum(forcing * forcing), 'flow')  40.9 us
    reduce_sum x3, other arithmetic, body(): local_terms = [jnp.sum(centre_image * vector) for vector in aligned]  22.2 us
    ppermute x4, starting transfers between devices, extended(): lax.ppermute(lax.slice_in_dim(block, block.shape[dim] - width, None, axis...  16.7 us
    ppermute x4, waiting for transfers between devices, extended(): lax.ppermute(lax.slice_in_dim(block, 0, width, axis=dim), axis, backward)  13.9 us
    ppermute x4, starting transfers between devices, extended(): lax.ppermute(lax.slice_in_dim(block, 0, width, axis=dim), axis, backward)  11.9 us
    div x2, other arithmetic, body(): krylov.append((image / new_norm, depth_to))  7.95 us
    unnamed x244, local copies, waits for them, and re-layouts  7.91 us
  transfers between devices with their start and end apart: 8, of which 7 were waited for; matrix products, arithmetic and copies ran while one was open for 5% of the time, Pallas kernels for 0%

commit v1 on v0

v1 whole, which is shorter than its diff:
```python
import functools

import jax
import jax.numpy as jnp
from jax import lax
from jax.experimental import pallas as pl
from jax.experimental.pallas import tpu as pltpu
from jax.sharding import PartitionSpec as P

ITERS = 3
epsilon = 1e-06
relaxation = 0.5
reach_weights = (1.0, 0.6, 0.35, 0.2)
REACH = len(reach_weights)
LANES = 128
SUB = 8
MESH = pl.DeviceIdType.MESH
PAIRS = tuple((i, j) for j in range(ITERS + 1) for i in range(j + 1))


def fold(x):
    lead, (rows, cols) = x.shape[:-2], x.shape[-2:]
    x = x.reshape(lead + (rows // SUB, SUB, cols // LANES, LANES))
    return jnp.swapaxes(x, -3, -2).reshape(lead + (rows * cols // LANES, LANES))


def unfold(x, rows, cols):
    lead = x.shape[:-2]
    x = x.reshape(lead + (rows // SUB, cols // LANES, SUB, LANES))
    return jnp.swapaxes(x, -3, -2).reshape(lead + (rows, cols))


def least_squares(columns, start):
    count_cols = len(columns)
    givens_rhs = [start] + [start * 0.0 for index in range(count_cols)]
    cosines, sines, upper_cols = ([], [], [])
    for column_index, column_in in enumerate(columns):
        column = list(column_in)
        for row in range(column_index):
            rotated_a = cosines[row] * column[row] + sines[row] * column[row + 1]
            rotated_b = -sines[row] * column[row] + cosines[row] * column[row + 1]
            column[row] = rotated_a
            column[row + 1] = rotated_b
        radius = jnp.sqrt(
            column[column_index] * column[column_index]
            + column[column_index + 1] * column[column_index + 1]
        )
        cosine = column[column_index] / radius
        sine_value = column[column_index + 1] / radius
        column[column_index] = radius
        cosines.append(cosine)
        sines.append(sine_value)
        upper_cols.append(column)
        next_rhs = -sine_value * givens_rhs[column_index]
        givens_rhs[column_index] = cosine * givens_rhs[column_index]
        givens_rhs[column_index + 1] = next_rhs
    factors = [None] * count_cols
    for column_index in range(count_cols - 1, -1, -1):
        accum = givens_rhs[column_index]
        for later in range(column_index + 1, count_cols):
            accum = accum - upper_cols[later][column_index] * factors[later]
        factors[column_index] = accum / upper_cols[column_index][column_index]
    return factors


def combine(gram):
    def inner(left, right):
        total = None
        for i, a in enumerate(left):
            for j, b in enumerate(right):
                term = a * b * gram[(min(i, j), max(i, j))]
                total = term if total is None else total + term
        return total

    load_norm = jnp.sqrt(gram[(0, 0)] + epsilon)
    krylov = [[1.0 / load_norm]]
    columns = []
    for j in range(ITERS):
        base = krylov[j]
        image = [base[0]]
        for i in range(1, j + 1):
            image.append(base[i] - base[i - 1])
        image.append(-base[j])
        column = []
        for vector in krylov:
            weight = inner(image, vector)
            image = [
                a - weight * vector[i] if i < len(vector) else a
                for i, a in enumerate(image)
            ]
            column.append(weight)
        new_norm = jnp.sqrt(jnp.maximum(inner(image, image), 0.0) + epsilon)
        column.append(new_norm)
        columns.append(column)
        krylov.append([a / new_norm for a in image])
    factors = least_squares(columns, load_norm)
    coefs = []
    for i in range(ITERS):
        total = None
        for j in range(i, ITERS):
            term = factors[j] * krylov[j][i]
            total = term if total is None else total + term
        coefs.append(total)
    rest = [1.0 - coefs[0]]
    for i in range(1, ITERS):
        rest.append(coefs[i - 1] - coefs[i])
    rest.append(coefs[ITERS - 1])
    return coefs, rest


def kernel(
    count, inner_group, rows, layers,
    f_ref, visc_ref, fric_ref, rot_ref, vert_ref, ice_ref, ground_ref,
    sol_ref, res_ref,
    S, B, ER, EI, LK, VN, ACC, SEND1, GOT1, SEND2, GOT2,
    halo_send, halo_recv, one_send, one_recv, two_send, two_recv,
):
    me = lax.axis_index("flow")
    planes = 2 * layers
    outer_group = count // inner_group
    mine_in = lax.rem(me, inner_group)
    mine_out = me // inner_group
    first = me - mine_in

    def inner_peer(d):
        return first + lax.rem(mine_in + d, inner_group)

    def outer_peer(d):
        return lax.rem(mine_out + d, outer_group) * inner_group + mine_in

    has_left = me > 0
    has_right = me < count - 1
    barrier = pltpu.get_barrier_semaphore()
    for d in range(1, inner_group):
        pl.semaphore_signal(barrier, inc=1, device_id=(inner_peer(d),), device_id_type=MESH)
    for d in range(1, outer_group):
        pl.semaphore_signal(barrier, inc=1, device_id=(outer_peer(d),), device_id_type=MESH)

    @pl.when(has_left)
    def _():
        pl.semaphore_signal(barrier, inc=1, device_id=(me - 1,), device_id_type=MESH)

    @pl.when(has_right)
    def _():
        pl.semaphore_signal(barrier, inc=1, device_id=(me + 1,), device_id_type=MESH)

    zero = jnp.zeros((SUB, LANES), jnp.float32)

    @pl.when(me == 0)
    def _():
        for j in range(ITERS):
            S[j, 0:REACH] = jnp.zeros((REACH, planes, SUB, LANES), jnp.float32)

    @pl.when(me == count - 1)
    def _():
        for j in range(ITERS):
            S[j, rows + REACH : rows + 2 * REACH] = jnp.zeros(
                (REACH, planes, SUB, LANES), jnp.float32
            )

    lane = lax.broadcasted_iota(jnp.int32, (SUB, LANES), 1)
    sub = lax.broadcasted_iota(jnp.int32, (SUB, LANES), 0)
    lane_first, lane_last = lane == 0, lane == LANES - 1
    sub_first, sub_last = sub == 0, sub == SUB - 1
    horiz_total = 2.0 * sum(reach_weights) + 2.0

    def at(x):
        return pl.ds((x // SUB) * (SUB * SUB) + lax.rem(x, SUB), SUB, stride=SUB)

    def eliminate(x, k, source, carry):
        former, latter = source
        if k > 0:
            link = LK[x, k - 1]
            former = former + link * carry[0]
            latter = latter + link * carry[1]
        real, imag = ER[x, k], EI[x, k]
        return real * former + imag * latter, real * latter - imag * former

    def substitute(j, x, result):
        former, latter = result
        for k in range(layers - 2, -1, -1):
            link = LK[x, k]
            former, latter = link * former, link * latter
            real, imag = ER[x, k], EI[x, k]
            former, latter = (
                S[j, x + REACH, k] + real * former + imag * latter,
                S[j, x + REACH, layers + k] + real * latter - imag * former,
            )
            S[j, x + REACH, k] = former
            S[j, x + REACH, layers + k] = latter

    def prepare(x):
        here = at(x)
        ice = ice_ref[here, :] > 0
        visc = visc_ref[here, :]
        drag = jnp.where(ground_ref[here, :] > 0, fric_ref[here, :], 0.0)
        imag_part = jnp.where(ice, rot_ref[here, :], 0.0)
        VN[x] = jnp.where(ice, visc, 0.0)
        above = zero
        real = imag = carry = None
        square = zero
        for k in range(layers):
            below = above
            above = vert_ref[k, here, :] if k < layers - 1 else zero
            part = above + below + relaxation * visc + horiz_total * visc
            if k == 0:
                part = part + drag
            pivot_real = jnp.where(ice, part, 1.0)
            pivot_imag = imag_part
            if k > 0:
                link = jnp.where(ice, below, 0.0)
                LK[x, k - 1] = link
                pivot_real = pivot_real - link * link * real
                pivot_imag = pivot_imag - link * link * imag
            inverse = 1.0 / (pivot_real * pivot_real + pivot_imag * pivot_imag)
            real = pivot_real * inverse
            imag = -pivot_imag * inverse
            ER[x, k] = real
            EI[x, k] = imag
            former, latter = f_ref[0, k, here, :], f_ref[1, k, here, :]
            B[0, x, k] = former
            B[0, x, layers + k] = latter
            square = square + (former * former + latter * latter)
            carry = eliminate(x, k, (former, latter), carry)
            S[0, x + REACH, k] = carry[0]
            S[0, x + REACH, layers + k] = carry[1]
        substitute(0, x, carry)
        ACC[0] = ACC[0] + square

    def advance(j, x):
        scale = VN[x]
        carry = None
        sums = [zero] * (j + 2)
        for k in range(layers):
            source = []
            for c in range(2):
                p = c * layers + k
                u = S[j, x + REACH, p]
                left = pltpu.roll(u, 1, 1)
                left = jnp.where(
                    lane_first, jnp.where(sub_first, 0.0, pltpu.roll(left, 1, 0)), left
                )
                right = pltpu.roll(u, LANES - 1, 1)
                right = jnp.where(
                    lane_last, jnp.where(sub_last, 0.0, pltpu.roll(right, SUB - 1, 0)), right
                )
                total = left + right
                for m, weight in enumerate(reach_weights):
                    total = total + weight * (
                        S[j, x + REACH + m + 1, p] + S[j, x + REACH - m - 1, p]
                    )
                b = scale * total
                B[j + 1, x, p] = b
                for i in range(j + 1):
                    sums[i] = sums[i] + b * B[i, x, p]
                sums[j + 1] = sums[j + 1] + b * b
                source.append(b)
            if j + 1 < ITERS:
                carry = eliminate(x, k, source, carry)
                S[j + 1, x + REACH, k] = carry[0]
                S[j + 1, x + REACH, layers + k] = carry[1]
        if j + 1 < ITERS:
            substitute(j + 1, x, carry)
        for i in range(j + 2):
            slot = PAIRS.index((i, j + 1))
            ACC[slot] = ACC[slot] + sums[i]

    def to_left(j, r):
        return pltpu.make_async_remote_copy(
            src_ref=S.at[j, REACH + r],
            dst_ref=S.at[j, REACH + rows + r],
            send_sem=halo_send.at[j, 0, r],
            recv_sem=halo_recv.at[j, 0, r],
            device_id=(me - 1,),
            device_id_type=MESH,
        )

    def to_right(j, r):
        return pltpu.make_async_remote_copy(
            src_ref=S.at[j, rows + r],
            dst_ref=S.at[j, r],
            send_sem=halo_send.at[j, 1, r],
            recv_sem=halo_recv.at[j, 1, r],
            device_id=(me + 1,),
            device_id_type=MESH,
        )

    def edges(j, produce):
        for i in range(REACH):
            low, high = i, REACH - 1 - i
            produce(low)

            @pl.when(has_left)
            def _(low=low):
                to_left(j, low).start()

            produce(rows - REACH + high)

            @pl.when(has_right)
            def _(high=high):
                to_right(j, high).start()

    ACC[...] = jnp.zeros_like(ACC)
    waits = (inner_group - 1) + (outer_group - 1)
    pl.semaphore_wait(
        barrier, waits + has_left.astype(jnp.int32) + has_right.astype(jnp.int32)
    )

    edges(0, prepare)
    pl.loop(REACH, rows - REACH)(prepare)
    for j in range(ITERS):
        pl.loop(REACH, rows - REACH)(functools.partial(advance, j))

        @pl.when(has_right)
        def _(j=j):
            for r in range(REACH):
                to_left(j, r).wait_recv()

        @pl.when(has_left)
        def _(j=j):
            for r in range(REACH):
                to_right(j, r).wait_recv()

        if j + 1 < ITERS:
            edges(j + 1, functools.partial(advance, j))
        else:
            pl.loop(0, REACH)(functools.partial(advance, j))
            pl.loop(rows - REACH, rows)(functools.partial(advance, j))

    SEND1[...] = jnp.zeros_like(SEND1)
    for slot in range(len(PAIRS)):
        SEND1[slot : slot + 1, :] = jnp.sum(ACC[slot], axis=0, keepdims=True)

    def exchange(size, peer, sent, got, send_sem, recv_sem):
        copies = []
        for d in range(1, size):
            copy = pltpu.make_async_remote_copy(
                src_ref=sent,
                dst_ref=got.at[d - 1],
                send_sem=send_sem.at[d - 1],
                recv_sem=recv_sem.at[d - 1],
                device_id=(peer(d),),
                device_id_type=MESH,
            )
            copy.start()
            copies.append(copy)
        for copy in copies:
            copy.wait_recv()
        return copies

    first_copies = exchange(inner_group, inner_peer, SEND1, GOT1, one_send, one_recv)
    total = SEND1[...]
    for d in range(1, inner_group):
        total = total + GOT1[d - 1]
    SEND2[...] = total
    second_copies = exchange(outer_group, outer_peer, SEND2, GOT2, two_send, two_recv)
    for d in range(1, outer_group):
        total = total + GOT2[d - 1]
    total = jnp.sum(total, axis=1, keepdims=True)
    gram = {pair: total[slot : slot + 1, :] for slot, pair in enumerate(PAIRS)}
    coefs, rest = combine(gram)
    coefs = [jnp.broadcast_to(a, (SUB, LANES)) for a in coefs]
    rest = [jnp.broadcast_to(a, (SUB, LANES)) for a in rest]

    def finish(x):
        here = at(x)
        for c in range(2):
            for k in range(layers):
                p = c * layers + k
                value = coefs[0] * S[0, x + REACH, p]
                for i in range(1, ITERS):
                    value = value + coefs[i] * S[i, x + REACH, p]
                sol_ref[c, k, here, :] = value
                value = rest[0] * B[0, x, p]
                for i in range(1, ITERS + 1):
                    value = value + rest[i] * B[i, x, p]
                res_ref[c, k, here, :] = value

    pl.loop(0, rows)(finish)

    for copy in first_copies + second_copies:
        copy.wait_send()
    for j in range(ITERS):

        @pl.when(has_left)
        def _(j=j):
            for r in range(REACH):
                to_left(j, r).wait_send()

        @pl.when(has_right)
        def _(j=j):
            for r in range(REACH):
                to_right(j, r).wait_send()


def body(count, forcing, viscosity, friction, rotation, vertical, ice_mask, grounded):
    comps, layers, rows, cols = forcing.shape
    planes = comps * layers
    inner_group = 8 if count % 8 == 0 else count
    outer_group = count // inner_group
    folded = [fold(a) for a in (forcing, viscosity, friction, rotation, vertical, ice_mask, grounded)]
    shape = jax.ShapeDtypeStruct(folded[0].shape, jnp.float32)
    slots = -(-len(PAIRS) // SUB) * SUB
    f32 = jnp.float32
    outs = pl.pallas_call(
        functools.partial(kernel, count, inner_group, rows, layers),
        out_shape=(shape, shape),
        in_specs=[pl.BlockSpec(memory_space=pltpu.VMEM)] * len(folded),
        out_specs=(pl.BlockSpec(memory_space=pltpu.VMEM),) * 2,
        scratch_shapes=[
            pltpu.VMEM((ITERS, rows + 2 * REACH, planes, SUB, LANES), f32),
            pltpu.VMEM((ITERS + 1, rows, planes, SUB, LANES), f32),
            pltpu.VMEM((rows, layers, SUB, LANES), f32),
            pltpu.VMEM((rows, layers, SUB, LANES), f32),
            pltpu.VMEM((rows, layers - 1, SUB, LANES), f32),
            pltpu.VMEM((rows, SUB, LANES), f32),
            pltpu.VMEM((len(PAIRS), SUB, LANES), f32),
            pltpu.VMEM((slots, LANES), f32),
            pltpu.VMEM((max(inner_group - 1, 1), slots, LANES), f32),
            pltpu.VMEM((slots, LANES), f32),
            pltpu.VMEM((max(outer_group - 1, 1), slots, LANES), f32),
            pltpu.SemaphoreType.DMA((ITERS, 2, REACH)),
            pltpu.SemaphoreType.DMA((ITERS, 2, REACH)),
            pltpu.SemaphoreType.DMA((max(inner_group - 1, 1),)),
            pltpu.SemaphoreType.DMA((max(inner_group - 1, 1),)),
            pltpu.SemaphoreType.DMA((max(outer_group - 1, 1),)),
            pltpu.SemaphoreType.DMA((max(outer_group - 1, 1),)),
        ],
        compiler_params=pltpu.CompilerParams(
            collective_id=0, has_side_effects=True, vmem_limit_bytes=60 * 1024 * 1024
        ),
    )(*folded)
    return tuple(unfold(a, rows, cols) for a in outs)


def solution(mesh):
    return jax.shard_map(
        functools.partial(body, mesh.shape["flow"]),
        mesh=mesh,
        in_specs=(
            P(None, None, "flow", None),
            P("flow", None),
            P("flow", None),
            P("flow", None),
            P(None, "flow", None),
            P("flow", None),
            P("flow", None),
        ),
        out_specs=(P(None, None, "flow", None), P(None, None, "flow", None)),
        check_vma=False,
    )
```

time: 327 us -> 57.8 us (0.18)
  the two profiles are of different devices: /device:TPU:1 before, /device:TPU:0 now
where the time goes in v1:
time: 57.8 us; the launch traced here: 57.6 us
  Pallas kernels  52 us (90%)
  local copies, waits for them, and re-layouts  4.92 us (9%)
  between operations  0.65 us (1%)
    pallas_call x1, Pallas kernels, body(): pl.pallas_call(functools.partial(kernel, count, inner_group, rows, layers...  52 us
    unnamed x4, local copies, waits for them, and re-layouts  4.92 us

profile of v1, /device:TPU:0, one launch (start us, length us, event | category | flops | bytes accessed | tf_op | source)
XLA Modules:
  0.0 57.6 jit_solution(13337440009980515922)
XLA Ops:
  0.6 52.0 %shard_map.86 = (f32[2,12,192,128]{3,2,1,0:T(8,128)}, f32[2,12,192,128]{3,2,1,0:T(8,128)}) custom-call(f32[2,12,192,128]{3,2,1,0:T(8,128)} %bitcast.47, f32[192,128]{1,0:T(8,128)} %bitcast.49, f32[192,128]{1,0:T(8,128)} %bitcast.50, f32[192,128]{1,0:T(8,128)} %bitcast.51, f32[11,192,128]{2,1,0:T(8,128)} %bitcast.48, s32[192,128]{1,0:T(8,128)} %bitcast.52, ...), custom_call_target="tpu_custom_call" | custom-call | tf_op jit(solution)/shard_map/pallas_call | solution.py:405
  52.7 0.0 copy-start
  52.7 3.5 %copy.11 = f32[2,12,24,1024]{3,2,1,0:T(8,128)} copy(f32[2,12,24,1024]{3,2,1,0:T(8,128)} %bitcast.46) | data formatting | bytes 4718592
  56.2 0.0 copy-done
  56.2 1.4 %copy.12 = f32[2,12,24,1024]{3,2,1,0:T(8,128)} copy(f32[2,12,24,1024]{3,2,1,0:T(8,128)S(1)} %bitcast.45) | data formatting | bytes 4718592
Async XLA Ops:
  52.7 3.5 %copy-start = (f32[2,12,192,128]{3,2,1,0:T(8,128)S(1)}, f32[2,12,192,128]{3,2,1,0:T(8,128)}, u32[]{:S(2)}) copy-start(f32[2,12,192,128]{3,2,1,0:T(8,128)} %get-tuple-element.5) | copy-start | bytes 7077892

commit v2 on v1

--- a/solution.py
+++ b/solution.py
@@ -14,6 +14,7 @@
 REACH = len(reach_weights)
 LANES = 128
 SUB = 8
+VMEM_BYTES = 67043328
 MESH = pl.DeviceIdType.MESH
 PAIRS = tuple((i, j) for j in range(ITERS + 1) for i in range(j + 1))
 
@@ -110,10 +111,11 @@
 
 def kernel(
     count, inner_group, rows, layers,
+    f_hbm, visc_hbm, fric_hbm, rot_hbm, vert_hbm, ice_hbm, ground_hbm,
+    sol_ref, res_ref,
     f_ref, visc_ref, fric_ref, rot_ref, vert_ref, ice_ref, ground_ref,
-    sol_ref, res_ref,
     S, B, ER, EI, LK, VN, ACC, SEND1, GOT1, SEND2, GOT2,
-    halo_send, halo_recv, one_send, one_recv, two_send, two_recv,
+    load_sem, halo_send, halo_recv, one_send, one_recv, two_send, two_recv,
 ):
     me = lax.axis_index("flow")
     planes = 2 * layers
@@ -127,6 +129,27 @@
 
     def outer_peer(d):
         return lax.rem(mine_out + d, outer_group) * inner_group + mine_in
+
+    tiles = rows // SUB
+    arguments = (
+        (f_hbm, f_ref), (visc_hbm, visc_ref), (fric_hbm, fric_ref), (rot_hbm, rot_ref),
+        (vert_hbm, vert_ref), (ice_hbm, ice_ref), (ground_hbm, ground_ref),
+    )
+
+    def loads(tile):
+        part = pl.ds(tile * SUB * SUB, SUB * SUB)
+        copies = []
+        for slot, (far, near) in enumerate(arguments):
+            place = (slice(None),) * (len(near.shape) - 2) + (part,)
+            copies.append(
+                pltpu.make_async_copy(far.at[place], near.at[place], load_sem.at[tile, slot])
+            )
+        return copies
+
+    tile_order = [0] + ([tiles - 1] if tiles > 1 else []) + list(range(1, tiles - 1))
+    for tile in tile_order:
+        for copy in loads(tile):
+            copy.start()
 
     has_left = me > 0
     has_right = me < count - 1
@@ -285,47 +308,55 @@
             device_id_type=MESH,
         )
 
-    def edges(j, produce):
+    waits = (inner_group - 1) + (outer_group - 1)
+    waits = waits + has_left.astype(jnp.int32) + has_right.astype(jnp.int32)
+
+    def edges(j, produce, outer_first):
         for i in range(REACH):
-            low, high = i, REACH - 1 - i
+            low = i if outer_first else REACH - 1 - i
+            high = REACH - 1 - low
+            if j > 0 and not outer_first:
+                arrive(j - 1, high, low)
             produce(low)
+            produce(rows - REACH + high)
+            if j == 0 and i == 0:
+                pl.semaphore_wait(barrier, waits)
+            if j == ITERS:
+                continue
 
             @pl.when(has_left)
             def _(low=low):
                 to_left(j, low).start()
 
-            produce(rows - REACH + high)
-
             @pl.when(has_right)
             def _(high=high):
                 to_right(j, high).start()
 
+    def arrive(j, from_right, from_left):
+        @pl.when(has_right)
+        def _():
+            to_left(j, from_right).wait_recv()
+
+        @pl.when(has_left)
+        def _():
+            to_right(j, from_left).wait_recv()
+
     ACC[...] = jnp.zeros_like(ACC)
-    waits = (inner_group - 1) + (outer_group - 1)
-    pl.semaphore_wait(
-        barrier, waits + has_left.astype(jnp.int32) + has_right.astype(jnp.int32)
-    )
-
-    edges(0, prepare)
+    for tile in tile_order[:2]:
+        for copy in loads(tile):
+            copy.wait()
+    edges(0, prepare, True)
+    for tile in tile_order[2:]:
+        for copy in loads(tile):
+            copy.wait()
     pl.loop(REACH, rows - REACH)(prepare)
     for j in range(ITERS):
         pl.loop(REACH, rows - REACH)(functools.partial(advance, j))
-
-        @pl.when(has_right)
-        def _(j=j):
+        outer_first = j % 2 == 1
+        if outer_first:
             for r in range(REACH):
-                to_left(j, r).wait_recv()
-
-        @pl.when(has_left)
-        def _(j=j):
-            for r in range(REACH):
-                to_right(j, r).wait_recv()
-
-        if j + 1 < ITERS:
-            edges(j + 1, functools.partial(advance, j))
-        else:
-            pl.loop(0, REACH)(functools.partial(advance, j))
-            pl.loop(rows - REACH, rows)(functools.partial(advance, j))
+                arrive(j, r, r)
+        edges(j + 1, functools.partial(advance, j), outer_first)
 
     SEND1[...] = jnp.zeros_like(SEND1)
     for slot in range(len(PAIRS)):
@@ -399,15 +430,17 @@
     inner_group = 8 if count % 8 == 0 else count
     outer_group = count // inner_group
     folded = [fold(a) for a in (forcing, viscosity, friction, rotation, vertical, ice_mask, grounded)]
-    shape = jax.ShapeDtypeStruct(folded[0].shape, jnp.float32)
+    shape = pltpu.VMEM(folded[0].shape, jnp.float32)
     slots = -(-len(PAIRS) // SUB) * SUB
     f32 = jnp.float32
+    room = 2 * 4 * forcing.size + 65536
     outs = pl.pallas_call(
         functools.partial(kernel, count, inner_group, rows, layers),
         out_shape=(shape, shape),
-        in_specs=[pl.BlockSpec(memory_space=pltpu.VMEM)] * len(folded),
+        in_specs=[pl.BlockSpec(memory_space=pltpu.HBM)] * len(folded),
         out_specs=(pl.BlockSpec(memory_space=pltpu.VMEM),) * 2,
-        scratch_shapes=[
+        scratch_shapes=[pltpu.VMEM(a.shape, a.dtype) for a in folded]
+        + [
             pltpu.VMEM((ITERS, rows + 2 * REACH, planes, SUB, LANES), f32),
             pltpu.VMEM((ITERS + 1, rows, planes, SUB, LANES), f32),
             pltpu.VMEM((rows, layers, SUB, LANES), f32),
@@ -419,6 +452,7 @@
             pltpu.VMEM((max(inner_group - 1, 1), slots, LANES), f32),
             pltpu.VMEM((slots, LANES), f32),
             pltpu.VMEM((max(outer_group - 1, 1), slots, LANES), f32),
+            pltpu.SemaphoreType.DMA((rows // SUB, len(folded))),
             pltpu.SemaphoreType.DMA((ITERS, 2, REACH)),
             pltpu.SemaphoreType.DMA((ITERS, 2, REACH)),
             pltpu.SemaphoreType.DMA((max(inner_group - 1, 1),)),
@@ -427,7 +461,7 @@
             pltpu.SemaphoreType.DMA((max(outer_group - 1, 1),)),
         ],
         compiler_params=pltpu.CompilerParams(
-            collective_id=0, has_side_effects=True, vmem_limit_bytes=60 * 1024 * 1024
+            collective_id=0, has_side_effects=True, vmem_limit_bytes=VMEM_BYTES - room
         ),
     )(*folded)
     return tuple(unfold(a, rows, cols) for a in outs)

time: 57.8 us -> 48.5 us (0.84)
  Pallas kernels: 52 us -> 44.9 us
  local copies, waits for them, and re-layouts: 4.92 us -> 2.81 us
    pallas_call x1, Pallas kernels: 52 us -> 44.9 us  [body(): pl.pallas_call(functools.partial(kernel, count, inner_group, rows, layers...]
    unnamed x4 -> x2, local copies, waits for them, and re-layouts: 4.92 us -> 2.81 us
where the time goes in v2:
time: 48.5 us; the launch traced here: 48.3 us
  Pallas kernels  44.9 us (93%)
  local copies, waits for them, and re-layouts  2.81 us (6%)
  between operations  0.64 us (1%)
    pallas_call x1, Pallas kernels, body(): pl.pallas_call(functools.partial(kernel, count, inner_group, rows, layers...  44.9 us
    unnamed x2, local copies, waits for them, and re-layouts  2.81 us

profile of v2, /device:TPU:0, one launch (start us, length us, event | category | flops | bytes accessed | tf_op | source)
XLA Modules:
  0.0 48.3 jit_solution(14808268273704646196)
XLA Ops:
  0.6 44.9 %shard_map.86 = (f32[2,12,192,128]{3,2,1,0:T(8,128)S(1)}, f32[2,12,192,128]{3,2,1,0:T(8,128)S(1)}) custom-call(f32[2,12,192,128]{3,2,1,0:T(8,128)} %bitcast.47, f32[192,128]{1,0:T(8,128)} %bitcast.49, f32[192,128]{1,0:T(8,128)} %bitcast.50, f32[192,128]{1,0:T(8,128)} %bitcast.51, f32[11,192,128]{2,1,0:T(8,128)} %bitcast.48, s32[192,128]{1,0:T(8,128)} %bitcast.52, ...), custom_call_target="tpu_custom_call" | custom-call | tf_op jit(solution)/shard_map/pallas_call | solution.py:437
  45.5 1.4 %copy.11 = f32[2,12,24,1024]{3,2,1,0:T(8,128)} copy(f32[2,12,24,1024]{3,2,1,0:T(8,128)S(1)} %bitcast.46) | data formatting | bytes 4718592
  46.9 1.4 %copy.12 = f32[2,12,24,1024]{3,2,1,0:T(8,128)} copy(f32[2,12,24,1024]{3,2,1,0:T(8,128)S(1)} %bitcast.45) | data formatting | bytes 4718592

commit v3 on v2

--- a/solution.py
+++ b/solution.py
@@ -114,10 +114,11 @@
     f_hbm, visc_hbm, fric_hbm, rot_hbm, vert_hbm, ice_hbm, ground_hbm,
     sol_ref, res_ref,
     f_ref, visc_ref, fric_ref, rot_ref, vert_ref, ice_ref, ground_ref,
-    S, B, ER, EI, LK, VN, ACC, SEND1, GOT1, SEND2, GOT2,
+    S0, S1, S2, B0, B1, B2, B3, ER, EI, LK, VN, ACC, SEND1, GOT1, SEND2, GOT2,
     load_sem, halo_send, halo_recv, one_send, one_recv, two_send, two_recv,
 ):
     me = lax.axis_index("flow")
+    S, B = (S0, S1, S2), (B0, B1, B2, B3)
     planes = 2 * layers
     outer_group = count // inner_group
     mine_in = lax.rem(me, inner_group)
@@ -172,12 +173,12 @@
     @pl.when(me == 0)
     def _():
         for j in range(ITERS):
-            S[j, 0:REACH] = jnp.zeros((REACH, planes, SUB, LANES), jnp.float32)
+            S[j][0:REACH] = jnp.zeros((REACH, planes, SUB, LANES), jnp.float32)
 
     @pl.when(me == count - 1)
     def _():
         for j in range(ITERS):
-            S[j, rows + REACH : rows + 2 * REACH] = jnp.zeros(
+            S[j][rows + REACH : rows + 2 * REACH] = jnp.zeros(
                 (REACH, planes, SUB, LANES), jnp.float32
             )
 
@@ -199,99 +200,112 @@
         real, imag = ER[x, k], EI[x, k]
         return real * former + imag * latter, real * latter - imag * former
 
-    def substitute(j, x, result):
-        former, latter = result
+    def substitute(j, xs, results):
         for k in range(layers - 2, -1, -1):
-            link = LK[x, k]
-            former, latter = link * former, link * latter
-            real, imag = ER[x, k], EI[x, k]
-            former, latter = (
-                S[j, x + REACH, k] + real * former + imag * latter,
-                S[j, x + REACH, layers + k] + real * latter - imag * former,
-            )
-            S[j, x + REACH, k] = former
-            S[j, x + REACH, layers + k] = latter
-
-    def prepare(x):
-        here = at(x)
-        ice = ice_ref[here, :] > 0
-        visc = visc_ref[here, :]
-        drag = jnp.where(ground_ref[here, :] > 0, fric_ref[here, :], 0.0)
-        imag_part = jnp.where(ice, rot_ref[here, :], 0.0)
-        VN[x] = jnp.where(ice, visc, 0.0)
-        above = zero
-        real = imag = carry = None
-        square = zero
+            for n, x in enumerate(xs):
+                former, latter = results[n]
+                link = LK[x, k]
+                former, latter = link * former, link * latter
+                real, imag = ER[x, k], EI[x, k]
+                former, latter = (
+                    S[j][x + REACH, k] + real * former + imag * latter,
+                    S[j][x + REACH, layers + k] + real * latter - imag * former,
+                )
+                S[j][x + REACH, k] = former
+                S[j][x + REACH, layers + k] = latter
+                results[n] = former, latter
+
+    def prepare(*xs):
+        count_rows = len(xs)
+        places = [at(x) for x in xs]
+        ices = [ice_ref[here, :] > 0 for here in places]
+        viscs = [visc_ref[here, :] for here in places]
+        imag_parts = [
+            jnp.where(ice, rot_ref[here, :], 0.0) for ice, here in zip(ices, places)
+        ]
+        for x, ice, visc in zip(xs, ices, viscs):
+            VN[x] = jnp.where(ice, visc, 0.0)
+        above = [zero] * count_rows
+        inv = [None] * count_rows
+        carry = [None] * count_rows
+        square = [zero] * count_rows
         for k in range(layers):
-            below = above
-            above = vert_ref[k, here, :] if k < layers - 1 else zero
-            part = above + below + relaxation * visc + horiz_total * visc
-            if k == 0:
-                part = part + drag
-            pivot_real = jnp.where(ice, part, 1.0)
-            pivot_imag = imag_part
-            if k > 0:
-                link = jnp.where(ice, below, 0.0)
-                LK[x, k - 1] = link
-                pivot_real = pivot_real - link * link * real
-                pivot_imag = pivot_imag - link * link * imag
-            inverse = 1.0 / (pivot_real * pivot_real + pivot_imag * pivot_imag)
-            real = pivot_real * inverse
-            imag = -pivot_imag * inverse
-            ER[x, k] = real
-            EI[x, k] = imag
-            former, latter = f_ref[0, k, here, :], f_ref[1, k, here, :]
-            B[0, x, k] = former
-            B[0, x, layers + k] = latter
-            square = square + (former * former + latter * latter)
-            carry = eliminate(x, k, (former, latter), carry)
-            S[0, x + REACH, k] = carry[0]
-            S[0, x + REACH, layers + k] = carry[1]
-        substitute(0, x, carry)
-        ACC[0] = ACC[0] + square
-
-    def advance(j, x):
-        scale = VN[x]
-        carry = None
-        sums = [zero] * (j + 2)
+            for n, x in enumerate(xs):
+                here, ice, visc = places[n], ices[n], viscs[n]
+                below = above[n]
+                above[n] = vert_ref[k, here, :] if k < layers - 1 else zero
+                part = above[n] + below + relaxation * visc + horiz_total * visc
+                if k == 0:
+                    part = part + jnp.where(ground_ref[here, :] > 0, fric_ref[here, :], 0.0)
+                pivot_real = jnp.where(ice, part, 1.0)
+                pivot_imag = imag_parts[n]
+                if k > 0:
+                    link = jnp.where(ice, below, 0.0)
+                    LK[x, k - 1] = link
+                    pivot_real = pivot_real - link * link * inv[n][0]
+                    pivot_imag = pivot_imag - link * link * inv[n][1]
+                inverse = 1.0 / (pivot_real * pivot_real + pivot_imag * pivot_imag)
+                inv[n] = pivot_real * inverse, -pivot_imag * inverse
+                ER[x, k], EI[x, k] = inv[n]
+                former, latter = f_ref[0, k, here, :], f_ref[1, k, here, :]
+                B[0][x, k] = former
+                B[0][x, layers + k] = latter
+                square[n] = square[n] + (former * former + latter * latter)
+                carry[n] = eliminate(x, k, (former, latter), carry[n])
+                S[0][x + REACH, k], S[0][x + REACH, layers + k] = carry[n]
+        substitute(0, xs, carry)
+        ACC[0] = ACC[0] + sum(square[1:], square[0])
+
+    def advance(j, *xs, close=False):
+        scales = [VN[x] for x in xs]
+        carry = [None] * len(xs)
+        sums = [[zero] * (j + 2) for x in xs]
         for k in range(layers):
-            source = []
+            source = [[] for x in xs]
             for c in range(2):
                 p = c * layers + k
-                u = S[j, x + REACH, p]
-                left = pltpu.roll(u, 1, 1)
-                left = jnp.where(
-                    lane_first, jnp.where(sub_first, 0.0, pltpu.roll(left, 1, 0)), left
-                )
-                right = pltpu.roll(u, LANES - 1, 1)
-                right = jnp.where(
-                    lane_last, jnp.where(sub_last, 0.0, pltpu.roll(right, SUB - 1, 0)), right
-                )
-                total = left + right
-                for m, weight in enumerate(reach_weights):
-                    total = total + weight * (
-                        S[j, x + REACH + m + 1, p] + S[j, x + REACH - m - 1, p]
+                seen = {}
+
+                def row(n, offset):
+                    key = ("all", n + offset) if close else (n, offset)
+                    if key not in seen:
+                        start = xs[0] + n if close else xs[n]
+                        seen[key] = S[j][start + REACH + offset, p]
+                    return seen[key]
+
+                for n, x in enumerate(xs):
+                    u = row(n, 0)
+                    left = pltpu.roll(u, 1, 1)
+                    left = jnp.where(
+                        lane_first, jnp.where(sub_first, 0.0, pltpu.roll(left, 1, 0)), left
                     )
-                b = scale * total
-                B[j + 1, x, p] = b
-                for i in range(j + 1):
-                    sums[i] = sums[i] + b * B[i, x, p]
-                sums[j + 1] = sums[j + 1] + b * b
-                source.append(b)
+                    right = pltpu.roll(u, LANES - 1, 1)
+                    right = jnp.where(
+                        lane_last, jnp.where(sub_last, 0.0, pltpu.roll(right, SUB - 1, 0)), right
+                    )
+                    total = left + right
+                    for m, weight in enumerate(reach_weights):
+                        total = total + weight * (row(n, m + 1) + row(n, -m - 1))
+                    b = scales[n] * total
+                    B[j + 1][x, p] = b
+                    for i in range(j + 1):
+                        sums[n][i] = sums[n][i] + b * B[i][x, p]
+                    sums[n][j + 1] = sums[n][j + 1] + b * b
+                    source[n].append(b)
             if j + 1 < ITERS:
-                carry = eliminate(x, k, source, carry)
-                S[j + 1, x + REACH, k] = carry[0]
-                S[j + 1, x + REACH, layers + k] = carry[1]
+                for n, x in enumerate(xs):
+                    carry[n] = eliminate(x, k, source[n], carry[n])
+                    S[j + 1][x + REACH, k], S[j + 1][x + REACH, layers + k] = carry[n]
         if j + 1 < ITERS:
-            substitute(j + 1, x, carry)
+            substitute(j + 1, xs, carry)
         for i in range(j + 2):
             slot = PAIRS.index((i, j + 1))
-            ACC[slot] = ACC[slot] + sums[i]
+            ACC[slot] = ACC[slot] + sum((a[i] for a in sums[1:]), sums[0][i])
 
     def to_left(j, r):
         return pltpu.make_async_remote_copy(
-            src_ref=S.at[j, REACH + r],
-            dst_ref=S.at[j, REACH + rows + r],
+            src_ref=S[j].at[REACH + r],
+            dst_ref=S[j].at[REACH + rows + r],
             send_sem=halo_send.at[j, 0, r],
             recv_sem=halo_recv.at[j, 0, r],
             device_id=(me - 1,),
@@ -300,8 +314,8 @@
 
     def to_right(j, r):
         return pltpu.make_async_remote_copy(
-            src_ref=S.at[j, rows + r],
-            dst_ref=S.at[j, r],
+            src_ref=S[j].at[rows + r],
+            dst_ref=S[j].at[r],
             send_sem=halo_send.at[j, 1, r],
             recv_sem=halo_recv.at[j, 1, r],
             device_id=(me + 1,),
@@ -317,8 +331,7 @@
             high = REACH - 1 - low
             if j > 0 and not outer_first:
                 arrive(j - 1, high, low)
-            produce(low)
-            produce(rows - REACH + high)
+            produce(low, rows - REACH + high)
             if j == 0 and i == 0:
                 pl.semaphore_wait(barrier, waits)
             if j == ITERS:
@@ -398,13 +411,13 @@
         for c in range(2):
             for k in range(layers):
                 p = c * layers + k
-                value = coefs[0] * S[0, x + REACH, p]
+                value = coefs[0] * S[0][x + REACH, p]
                 for i in range(1, ITERS):
-                    value = value + coefs[i] * S[i, x + REACH, p]
+                    value = value + coefs[i] * S[i][x + REACH, p]
                 sol_ref[c, k, here, :] = value
-                value = rest[0] * B[0, x, p]
+                value = rest[0] * B[0][x, p]
                 for i in range(1, ITERS + 1):
-                    value = value + rest[i] * B[i, x, p]
+                    value = value + rest[i] * B[i][x, p]
                 res_ref[c, k, here, :] = value
 
     pl.loop(0, rows)(finish)
@@ -441,8 +454,8 @@
         out_specs=(pl.BlockSpec(memory_space=pltpu.VMEM),) * 2,
         scratch_shapes=[pltpu.VMEM(a.shape, a.dtype) for a in folded]
         + [
-            pltpu.VMEM((ITERS, rows + 2 * REACH, planes, SUB, LANES), f32),
-            pltpu.VMEM((ITERS + 1, rows, planes, SUB, LANES), f32),
+            *[pltpu.VMEM((rows + 2 * REACH, planes, SUB, LANES), f32)] * ITERS,
+            *[pltpu.VMEM((rows, planes, SUB, LANES), f32)] * (ITERS + 1),
             pltpu.VMEM((rows, layers, SUB, LANES), f32),
             pltpu.VMEM((rows, layers, SUB, LANES), f32),
             pltpu.VMEM((rows, layers - 1, SUB, LANES), f32),

time: 48.5 us -> 48.5 us (level)
  no operation moved by 1% of the time
where the time goes in v3:
time: 48.5 us; the launch traced here: 48.3 us
  Pallas kernels  44.9 us (93%)
  local copies, waits for them, and re-layouts  2.81 us (6%)
  between operations  0.64 us (1%)
    pallas_call x1, Pallas kernels, body(): pl.pallas_call(functools.partial(kernel, count, inner_group, rows, layers...  44.9 us
    unnamed x2, local copies, waits for them, and re-layouts  2.81 us

profile of v3, /device:TPU:0, one launch (start us, length us, event | category | flops | bytes accessed | tf_op | source)
XLA Modules:
  0.0 48.3 jit_solution(7483853292947269531)
XLA Ops:
  0.6 44.9 %shard_map.86 = (f32[2,12,192,128]{3,2,1,0:T(8,128)S(1)}, f32[2,12,192,128]{3,2,1,0:T(8,128)S(1)}) custom-call(f32[2,12,192,128]{3,2,1,0:T(8,128)} %bitcast.47, f32[192,128]{1,0:T(8,128)} %bitcast.49, f32[192,128]{1,0:T(8,128)} %bitcast.50, f32[192,128]{1,0:T(8,128)} %bitcast.51, f32[11,192,128]{2,1,0:T(8,128)} %bitcast.48, s32[192,128]{1,0:T(8,128)} %bitcast.52, ...), custom_call_target="tpu_custom_call" | custom-call | tf_op jit(solution)/shard_map/pallas_call | solution.py:450
  45.5 1.4 %copy.11 = f32[2,12,24,1024]{3,2,1,0:T(8,128)} copy(f32[2,12,24,1024]{3,2,1,0:T(8,128)S(1)} %bitcast.46) | data formatting | bytes 4718592
  46.9 1.4 %copy.12 = f32[2,12,24,1024]{3,2,1,0:T(8,128)} copy(f32[2,12,24,1024]{3,2,1,0:T(8,128)S(1)} %bitcast.45) | data formatting | bytes 4718592
